TPU v7x, 32 devices: a whole 2x2x4 slice. The times are simulated.
32 devices in a mesh: grp: 4 (over y, x), sub: 8 (over z, core).
Axes of the slice: x: 2, y: 2, z: 4, core: 2. Of those that a mesh axis runs over, the one named last changes fastest.
Arguments:
- right_side: float32 [24576, 160], P(('grp', 'sub')), may hold values from -6 to 6
- iterate_in: float32 [24576, 160], P(('grp', 'sub')), may hold values from -6 to 6
- diagonal: float32 [24576], P(('grp', 'sub')), may hold values from 1.5 to 4
- block_values: bfloat16 [32, 6, 3, 128, 128], P(('grp', 'sub')), may hold values from -0.125 to 0.125
- block_cols: int32 [32, 6, 3], P(('grp', 'sub')), may hold values from 0 to 5, as said below
- couple_left: bfloat16 [24576, 128], P(('grp', 'sub')), may hold values from -0.125 to 0.125
- couple_right: bfloat16 [24576, 128], P(('grp', 'sub')), may hold values from -0.125 to 0.125
- send_rows: int32 [32, 2, 128], P(('grp', 'sub')), may hold values from 0 to 767, as said below
- local_inverse: bfloat16 [32, 1024, 1024], P(('grp', 'sub')), may hold values from -0.3 to 2.3, as said below
- coarse_basis: bfloat16 [32, 1024, 32], P(('grp', 'sub')), may hold values from -0.1875 to 0.1875
- coarse_diag: float32 [32, 32, 32], P(('grp', 'sub')), may hold values from -54 to 59.5, as said below
- coarse_up: float32 [32, 32, 32], P(('grp', 'sub')), may hold values from -29.7 to 27
Outputs:
- iterate: float32 [24576, 160], P(('grp', 'sub'))
- residual: float32 [24576, 160], P(('grp', 'sub'))
Inputs may be any that keep to these rules, and one draw needn't show every extreme that they name: `block_cols`: the 3 column blocks of one row block are distinct. `send_rows`: the 256 rows listed for one subdomain are distinct. `local_inverse`: each block is symmetric positive definite. `coarse_diag`: each block is symmetric; with coarse_up the coarse operator is symmetric positive definite.
All inputs are finite; a program needn't handle non-finite values.
Results may differ from a plain program's by a relative error of at most 0.0032.
Values may be sent and summed in bfloat16 or wider, within the bound.
No kernel may reach another device: no remote copies, remote signals or barrier semaphores. Data moves between devices by JAX's collectives and lax.ppermute only.
A program may use at most 64 MiB of HBM per device.

v0:
```python
import jax
import jax.numpy as jnp
from jax import lax
from jax.sharding import PartitionSpec as P


def with_halo(cells, sides, width):
    for axis, dim in sides:
        count = lax.axis_size(axis)
        ends = count - 1
        head = lax.slice_in_dim(cells, 0, width, axis=dim)
        tail = lax.slice_in_dim(cells, cells.shape[dim] - width, cells.shape[dim], axis=dim)
        cells = jnp.concatenate(
            [
                lax.ppermute(tail, axis, [(i, (i + 1) % count) for i in range(ends)]),
                cells,
                lax.ppermute(head, axis, [((i + 1) % count, i) for i in range(ends)]),
            ],
            axis=dim,
        )
    return cells


def chol_solve(factor, values):
    halfway = lax.linalg.triangular_solve(factor, values, left_side=True, lower=True)
    return lax.linalg.triangular_solve(
        factor, halfway, left_side=True, lower=True, transpose_a=True
    )


def solve_chain(diagonal_blocks, upper, values):
    highest = lax.Precision.HIGHEST
    blocks_total = diagonal_blocks.shape[0]
    padded_total = 1
    while padded_total < blocks_total:
        padded_total = padded_total * 2
    extra = padded_total - blocks_total
    block_width = diagonal_blocks.shape[1]
    identity = jnp.eye(block_width, dtype=jnp.float32)
    diag_now = jnp.concatenate(
        [diagonal_blocks, jnp.broadcast_to(identity, (extra, block_width, block_width))], axis=0
    )
    upper_now = jnp.concatenate(
        [upper[:-1], jnp.zeros((extra + 1, block_width, block_width), jnp.float32)], axis=0
    )
    rhs_now = jnp.concatenate([values, jnp.zeros((extra,) + values.shape[1:], jnp.float32)], axis=0)
    levels = []
    while diag_now.shape[0] > 1:
        diag_even = diag_now[0::2]
        diag_odd = diag_now[1::2]
        upper_even = upper_now[0::2]
        upper_odd = upper_now[1::2]
        rhs_even = rhs_now[0::2]
        rhs_odd = rhs_now[1::2]
        factor = jnp.linalg.cholesky(diag_odd)
        stacked = jnp.concatenate([jnp.swapaxes(upper_even, 1, 2), upper_odd, rhs_odd], axis=2)
        through = chol_solve(factor, stacked)
        toward_left = through[:, :, :block_width]
        toward_right = through[:, :, block_width : 2 * block_width]
        odd_loads = through[:, :, 2 * block_width :]
        new_diag = diag_even - jnp.einsum(
            "mab,mbc->mac", upper_even, toward_left, precision=highest
        )
        new_upper = -jnp.einsum("mab,mbc->mac", upper_even, toward_right, precision=highest)
        new_rhs = rhs_even - jnp.einsum("mab,mbn->man", upper_even, odd_loads, precision=highest)
        from_diag = jnp.einsum("mba,mbc->mac", upper_odd, toward_right, precision=highest)
        from_rhs = jnp.einsum("mba,mbn->man", upper_odd, odd_loads, precision=highest)
        new_diag = new_diag - jnp.concatenate(
            [jnp.zeros_like(from_diag[:1]), from_diag[:-1]], axis=0
        )
        new_rhs = new_rhs - jnp.concatenate([jnp.zeros_like(from_rhs[:1]), from_rhs[:-1]], axis=0)
        levels.append((toward_left, toward_right, odd_loads))
        diag_now, upper_now, rhs_now = (new_diag, new_upper, new_rhs)
    solution = chol_solve(jnp.linalg.cholesky(diag_now[0]), rhs_now[0])[None]
    for toward_left, toward_right, odd_loads in reversed(levels):
        next_sol = jnp.concatenate([solution[1:], jnp.zeros_like(solution[:1])], axis=0)
        odd_part = (
            odd_loads
            - jnp.einsum("mab,mbn->man", toward_left, solution, precision=highest)
            - jnp.einsum("mab,mbn->man", toward_right, next_sol, precision=highest)
        )
        solution = jnp.stack([solution, odd_part], axis=1).reshape((-1,) + solution.shape[1:])
    return solution[:blocks_total]


def shards(
    right_side,
    iterate_in,
    diagonal,
    block_values,
    block_cols,
    couple_left,
    couple_right,
    send_rows,
    local_inverse,
    coarse_basis,
    coarse_diag,
    coarse_up,
):
    bf16 = jnp.bfloat16
    f32 = jnp.float32
    highest = lax.Precision.HIGHEST
    intersection = send_rows.shape[2]
    rows_own = right_side.shape[0]
    cases = right_side.shape[1]
    row_blocks = block_cols.shape[1]
    modes = coarse_basis.shape[2]
    column_blocks = block_cols[0]
    sent_left_rows = send_rows[0, 0]
    sent_right_rows = send_rows[0, 1]

    def neighbour_rows(source):
        boundary = jnp.stack([source[sent_left_rows], source[sent_right_rows]])
        padded = with_halo(boundary, ((("grp", "sub"), 0),), 1)
        return (padded[0], padded[3])

    def apply_operator(vector):
        rounded = vector.astype(bf16)
        from_left, from_right = neighbour_rows(rounded)
        blocks = rounded.reshape(row_blocks, -1, cases)
        picked = blocks[column_blocks]
        sparse = jnp.einsum(
            "itab,itbn->ian", block_values[0], picked, preferred_element_type=f32
        ).reshape(rows_own, cases)
        coupled = jnp.dot(couple_left, from_left, preferred_element_type=f32) + jnp.dot(
            couple_right, from_right, preferred_element_type=f32
        )
        return diagonal[:, None] * vector + (sparse + coupled)

    residual_start = right_side - apply_operator(iterate_in)
    rounded = residual_start.astype(bf16)
    from_left, from_right = neighbour_rows(rounded)
    extended = jnp.concatenate([from_left, rounded, from_right], axis=0)
    local_part = jnp.dot(local_inverse[0], extended, preferred_element_type=f32)
    coarse_in = jnp.dot(coarse_basis[0].T, extended, preferred_element_type=f32)
    blocks_diag = lax.all_gather(coarse_diag, "sub", axis=0, tiled=True)
    blocks_up = lax.all_gather(coarse_up, "sub", axis=0, tiled=True)
    group = lax.axis_index("grp")
    groups = lax.axis_size("grp")
    member = lax.axis_index("sub")
    members = lax.axis_size("sub")
    keep = (group < groups - 1).astype(f32)
    first_up = blocks_up[0]
    last_up = blocks_up[members - 1] * keep
    columns = lax.all_gather(coarse_in[None], "sub", axis=0, tiled=True)
    width = columns.shape[2]
    inner_count = members - 1
    empty_cols = jnp.zeros((inner_count, modes, modes), f32)
    left_cols = empty_cols.at[0].set(first_up.T)
    right_cols = empty_cols.at[inner_count - 1].set(last_up)
    stacked = jnp.concatenate([columns[1:], left_cols, right_cols], axis=2)
    solved = solve_chain(blocks_diag[1:], blocks_up[1:], stacked)
    sol_loads = solved[:, :, :width]
    sol_left = solved[:, :, width : width + modes]
    sol_right = solved[:, :, width + modes :]
    self_left = jnp.dot(first_up, sol_left[0], precision=highest)
    cross_term = jnp.dot(first_up, sol_right[0], precision=highest)
    rhs_first = jnp.dot(first_up, sol_loads[0], precision=highest)
    self_right = jnp.dot(last_up.T, sol_right[-1], precision=highest)
    rhs_last = jnp.dot(last_up.T, sol_loads[-1], precision=highest)
    sep_diag = lax.all_gather(blocks_diag[0][None], "grp", axis=0, tiled=True)
    sep_rhs = lax.all_gather(columns[0][None], "grp", axis=0, tiled=True)
    all_left = lax.all_gather(self_left[None], "grp", axis=0, tiled=True)
    all_right = lax.all_gather(self_right[None], "grp", axis=0, tiled=True)
    all_cross = lax.all_gather(cross_term[None], "grp", axis=0, tiled=True)
    all_first = lax.all_gather(rhs_first[None], "grp", axis=0, tiled=True)
    all_last = lax.all_gather(rhs_last[None], "grp", axis=0, tiled=True)
    prev_right = jnp.concatenate([jnp.zeros_like(all_right[:1]), all_right[:-1]], axis=0)
    prev_last = jnp.concatenate([jnp.zeros_like(all_last[:1]), all_last[:-1]], axis=0)
    reduced_diag = sep_diag - all_left - prev_right
    reduced_rhs = sep_rhs - all_first - prev_last
    sep_sol = solve_chain(reduced_diag, -all_cross, reduced_rhs)
    padded_sol = jnp.concatenate([sep_sol, jnp.zeros_like(sep_sol[:1])], axis=0)
    mine = lax.dynamic_index_in_dim(padded_sol, group, 0, keepdims=False)
    after = lax.dynamic_index_in_dim(padded_sol, group + 1, 0, keepdims=False)
    inner_sol = (
        sol_loads
        - jnp.einsum("ivw,wn->ivn", sol_left, mine, precision=highest)
        - jnp.einsum("ivw,wn->ivn", sol_right, after, precision=highest)
    )
    group_sol = jnp.concatenate([mine[None], inner_sol], axis=0)
    coarse_sol = lax.dynamic_index_in_dim(group_sol, member, 0, keepdims=False)
    correction = local_part + jnp.dot(
        coarse_basis[0], coarse_sol.astype(bf16), preferred_element_type=f32
    )
    tails = jnp.stack([correction[:intersection], correction[intersection + rows_own :]])
    returned = with_halo(tails.astype(jnp.bfloat16), ((("grp", "sub"), 0),), 1).astype(tails.dtype)
    owned = correction[intersection : intersection + rows_own]
    owned = owned.at[sent_right_rows].add(returned[3])
    owned = owned.at[sent_left_rows].add(returned[0])
    inner = lax.psum(jnp.sum(residual_start * owned, axis=0), ("grp", "sub"))
    image = apply_operator(owned)
    curvature = lax.psum(jnp.sum(owned * image, axis=0), ("grp", "sub"))
    step_size = inner / curvature
    return (iterate_in + step_size * owned, residual_start - step_size * image)


def solution(mesh):
    in_specs = (
        P(("grp", "sub"), None),
        P(("grp", "sub"), None),
        P(("grp", "sub")),
        P(("grp", "sub"), None, None, None, None),
        P(("grp", "sub"), None, None),
        P(("grp", "sub"), None),
        P(("grp", "sub"), None),
        P(("grp", "sub"), None, None),
        P(("grp", "sub"), None, None),
        P(("grp", "sub"), None, None),
        P(("grp", "sub"), None, None),
        P(("grp", "sub"), None, None),
    )
    out_specs = (P(("grp", "sub"), None), P(("grp", "sub"), None))
    return jax.shard_map(shards, mesh=mesh, in_specs=in_specs, out_specs=out_specs, check_vma=False)
```

profile of v0, /device:TPU:14, one launch (start us, length us, event | category | flops | bytes accessed | tf_op | source)
XLA Modules:
  0.0 289.2 jit_solution(11546375033526299166)
XLA Ops:
  0.7 1.3 copy.175
  2.8 1.5 gather_fusion.2
  4.3 1.9 collective-permute-start.1
  6.2 1.5 gather_fusion.1
  7.7 2.4 collective-permute-start
  10.4 14.8 %all_gather.32 = f32[8,32,32]{2,1,0:T(8,128)S(1)} all-gather(f32[1,32,32]{2,1,0:T(8,128)S(1)} %copy-done.34), channel_id=1, replica_groups=mesh['grp'=4,'sub'=8] {'sub'}, dimensions={0}, use_global_device_ids=true | all-gather | bytes 36864 | tf_op jit(solution)/shard_map/all_gather | solution.py:137
  25.2 14.0 %all_gather.30 = f32[8,32,32]{2,1,0:T(8,128)S(1)} all-gather(f32[1,32,32]{2,1,0:T(8,128)S(1)} %copy-done.35), channel_id=1, replica_groups=mesh['grp'=4,'sub'=8] {'sub'}, dimensions={0}, use_global_device_ids=true | all-gather | bytes 36864 | tf_op jit(solution)/shard_map/all_gather | solution.py:136
  39.5 11.7 %custom-call.47 = f32[4,32,32]{2,1,0:T(8,128)S(1)} custom-call(f32[4,32,32]{2,1,0:T(8,128)S(1)} %copy.185), custom_call_target="Cholesky" | custom-call | tf_op jit(solution)/shard_map/jit(cholesky)/cholesky | solution.py:55
  51.9 1.7 gather_fusion
  53.8 1.9 convolution_bitcast_fusion.1
  57.5 1.9 fusion.211
  59.6 1.1 gather_fusion.4
  61.8 4.0 %collective-permute-start.3 = (bf16[1,128,160]{1,2,0:T(8,128)(2,1)S(1)}, bf16[1,128,160]{1,2,0:T(8,128)(2,1)S(1)}, u32[]{:S(2)}, u32[]{:S(2)}) collective-permute-start(bf16[1,128,160]{1,2,0:T(8,128)(2,1)S(1)} %bitcast.412), channel_id=1, source_target_pairs={{1,0},{2,1},{3,2},{4,3},{5,4},{6,5},{7,6},{8,7},{9,8},{10,9},{11,1... | collective-permute-start | bytes 122888 | tf_op jit(solution)/shard_map/ppermute | solution.py:17
  65.9 1.9 collective-permute-start.2
  68.7 11.2 %custom-call.48 = f32[4,1,32,32]{2,3,1,0:T(8,128)} custom-call(f32[4,1,32,32]{3,2,1,0:T(8,128)} %select_bitcast_fusion), custom_call_target="InvertDiagBlocksLowerTriangular" | custom-call | tf_op jit(solution)/shard_map/triangular_solve | solution.py:26
  79.9 9.1 %all_gather.31 = f32[4,32,32]{2,1,0:T(8,128)S(1)} all-gather(f32[1,32,32]{2,1,0:T(8,128)S(1)} %slice-done.1), channel_id=1, replica_groups=mesh['grp'=4,'sub'=8] {'grp'}, dimensions={0}, use_global_device_ids=true | all-gather | bytes 20480 | tf_op jit(solution)/shard_map/all_gather | solution.py:161
  90.5 12.7 %all-gather = f32[256,160]{1,0:T(8,128)S(1)} all-gather(f32[32,160]{1,0:T(8,128)S(1)} %convolution_bitcast_fusion.11), channel_id=2, replica_groups=mesh['grp'=4,'sub'=8] {'sub'}, dimensions={0}, use_global_device_ids=true | all-gather | bytes 184320 | tf_op jit(solution)/shard_map/all_gather | solution.py:145
  106.0 5.9 %custom-call.57 = f32[2,32,32]{2,1,0:T(8,128)S(1)} custom-call(f32[2,32,32]{2,1,0:T(8,128)S(1)} %fusion.117), custom_call_target="Cholesky" | custom-call | tf_op jit(solution)/shard_map/jit(cholesky)/cholesky | solution.py:55
  112.1 4.9 %custom-call.49 = f32[2,1,32,32]{2,3,1,0:T(8,128)S(1)} custom-call(f32[2,1,32,32]{3,2,1,0:T(8,128)S(1)} %fusion.119), custom_call_target="InvertDiagBlocksLowerTriangular" | custom-call | tf_op jit(solution)/shard_map/triangular_solve | solution.py:26
  119.1 2.9 %custom-call.58 = f32[1,32,32]{2,1,0:T(8,128)S(1)} custom-call(f32[1,32,32]{2,1,0:T(8,128)S(1)} %fusion.169), custom_call_target="Cholesky" | custom-call | tf_op jit(solution)/shard_map/jit(cholesky)/cholesky | solution.py:55
  123.2 2.4 custom-call.50
  126.9 2.9 %cholesky.184 = f32[32,32]{1,0:T(8,128)S(1)} custom-call(f32[32,32]{1,0:T(8,128)S(1)} %fusion.150), custom_call_target="Cholesky" | custom-call | tf_op jit(solution)/shard_map/jit(cholesky)/cholesky | solution.py:74
  131.1 2.4 custom-call.51
  136.5 7.0 %all-gather.6 = f32[128,160]{1,0:T(8,128)S(1)} all-gather(f32[32,160]{1,0:T(8,128)S(1)} %slice-done), channel_id=8, replica_groups=mesh['grp'=4,'sub'=8] {'grp'}, dimensions={0}, use_global_device_ids=true | all-gather | bytes 102400 | tf_op jit(solution)/shard_map/all_gather | solution.py:162
  143.4 8.9 %all-gather.4 = f32[128,160]{1,0:T(8,128)S(1)} all-gather(f32[32,160]{1,0:T(8,128)S(1)} %convolution_bitcast_fusion.7), channel_id=6, replica_groups=mesh['grp'=4,'sub'=8] {'grp'}, dimensions={0}, use_global_device_ids=true | all-gather | bytes 102400 | tf_op jit(solution)/shard_map/all_gather | solution.py:166
  152.4 7.1 %all-gather.5 = f32[128,160]{1,0:T(8,128)S(1)} all-gather(f32[32,160]{1,0:T(8,128)S(1)} %fusion.101), channel_id=7, replica_groups=mesh['grp'=4,'sub'=8] {'grp'}, dimensions={0}, use_global_device_ids=true | all-gather | bytes 102400 | tf_op jit(solution)/shard_map/all_gather | solution.py:167
  159.6 8.7 %all-gather.3 = f32[128,32]{1,0:T(8,128)S(1)} all-gather(f32[32,32]{1,0:T(8,128)S(1)} %copy.214), channel_id=5, replica_groups=mesh['grp'=4,'sub'=8] {'grp'}, dimensions={0}, use_global_device_ids=true | all-gather | bytes 20480 | tf_op jit(solution)/shard_map/all_gather | solution.py:165
  168.5 6.7 %all-gather.2 = f32[128,32]{1,0:T(8,128)S(1)} all-gather(f32[32,32]{1,0:T(8,128)S(1)} %fusion.145), channel_id=4, replica_groups=mesh['grp'=4,'sub'=8] {'grp'}, dimensions={0}, use_global_device_ids=true | all-gather | bytes 20480 | tf_op jit(solution)/shard_map/all_gather | solution.py:164
  175.4 8.9 %all-gather.1 = f32[128,32]{1,0:T(8,128)S(1)} all-gather(f32[32,32]{1,0:T(8,128)S(1)} %copy.208), channel_id=3, replica_groups=mesh['grp'=4,'sub'=8] {'grp'}, dimensions={0}, use_global_device_ids=true | all-gather | bytes 20480 | tf_op jit(solution)/shard_map/all_gather | solution.py:163
  184.6 5.9 %custom-call.59 = f32[2,32,32]{2,1,0:T(8,128)S(1)} custom-call(f32[2,32,32]{2,1,0:T(8,128)S(1)} %fusion.112), custom_call_target="Cholesky" | custom-call | tf_op jit(solution)/shard_map/jit(cholesky)/cholesky | solution.py:55
  190.7 4.9 %custom-call.52 = f32[2,1,32,32]{2,3,1,0:T(8,128)S(1)} custom-call(f32[2,1,32,32]{3,2,1,0:T(8,128)S(1)} %fusion.118), custom_call_target="InvertDiagBlocksLowerTriangular" | custom-call | tf_op jit(solution)/shard_map/triangular_solve | solution.py:26
  197.6 2.9 %custom-call.60 = f32[1,32,32]{2,1,0:T(8,128)S(1)} custom-call(f32[1,32,32]{2,1,0:T(8,128)S(1)} %fusion.158), custom_call_target="Cholesky" | custom-call | tf_op jit(solution)/shard_map/jit(cholesky)/cholesky | solution.py:55
  201.9 2.4 custom-call.53
  205.5 2.9 %cholesky.216 = f32[32,32]{1,0:T(8,128)S(1)} custom-call(f32[32,32]{1,0:T(8,128)S(1)} %fusion.149), custom_call_target="Cholesky" | custom-call | tf_op jit(solution)/shard_map/jit(cholesky)/cholesky | solution.py:74
  209.8 2.4 custom-call.54
  215.4 1.9 collective-permute-start.5
  217.3 2.4 collective-permute-start.4
  220.1 4.3 %collective-permute-done.4 = bf16[1,128,160]{1,2,0:T(8,128)(2,1)S(1)} collective-permute-done((bf16[1,128,160]{1,2,0:T(8,128)(2,1)S(1)}, bf16[1,128,160]{1,2,0:T(8,128)(2,1)S(1)}, u32[]{:S(2)}, u32[]{:S(2)}) %collective-permute-start.4) | collective-permute-done | bytes 40992 | tf_op jit(solution)/shard_map/ppermute | solution.py:15
  224.6 1.6 scatter_fusion
  226.2 1.6 scatter_fusion.1
  228.9 1.6 gather_fusion.7
  231.4 1.9 collective-permute-start.7
  233.4 2.4 collective-permute-start.6
  236.8 1.5 convolution_bitcast_fusion
  238.6 3.1 %collective-permute-done.6 = bf16[1,128,160]{2,1,0:T(8,128)(2,1)S(1)} collective-permute-done((bf16[1,128,160]{2,1,0:T(8,128)(2,1)S(1)}, bf16[1,128,160]{2,1,0:T(8,128)(2,1)S(1)}, u32[]{:S(2)}, u32[]{:S(2)}) %collective-permute-start.6) | collective-permute-done | bytes 40992 | tf_op jit(solution)/shard_map/ppermute | solution.py:15
  241.7 1.1 multiply_reduce_fusion
  242.8 44.1 %all-reduce.16 = (f32[160]{0:T(256)S(1)}, f32[160]{0:T(256)S(1)}) all-reduce(f32[160]{0:T(256)S(1)} %get-tuple-element.30, f32[160]{0:T(256)S(1)} %get-tuple-element.29), channel_id=1, replica_groups=mesh['grp'=4,'sub'=8] {'grp','sub'}, use_global_device_ids=true, to_apply=%region_11.15 | all-reduce | flops 320 | bytes 2560 | tf_op jit(solution)/shard_map/psum | solution.py:191
  286.9 2.3 multiply_subtract_fusion
  (266 shorter events, 32.2 us)
Async XLA Ops:
  0.6 213.9 %copy-start = (bf16[1,1024,1024]{2,1,0:T(8,128)(2,1)S(1)}, bf16[1,1024,1024]{2,1,0:T(8,128)(2,1)}, u32[]{:S(2)}) copy-start(bf16[1,1024,1024]{2,1,0:T(8,128)(2,1)} %param.27) | copy-start | bytes 6291460
  0.6 9.5 %copy-start.43 = (s32[1,6,3]{1,0,2:T(1,128)S(1)}, s32[1,6,3]{1,0,2:T(1,128)}, u32[]{:S(2)}) copy-start(s32[1,6,3]{1,0,2:T(1,128)} %param.23) | copy-start | bytes 220
  0.7 9.7 %copy-start.34 = (f32[1,32,32]{2,1,0:T(8,128)S(1)}, f32[1,32,32]{2,1,0:T(8,128)}, u32[]{:S(2)}) copy-start(f32[1,32,32]{2,1,0:T(8,128)} %param.30) | copy-start | bytes 12292
  0.7 24.5 %copy-start.35 = (f32[1,32,32]{2,1,0:T(8,128)S(1)}, f32[1,32,32]{2,1,0:T(8,128)}, u32[]{:S(2)}) copy-start(f32[1,32,32]{2,1,0:T(8,128)} %param.29) | copy-start | bytes 12292
  2.8 7.3 %copy-start.38 = (s32[128]{0:T(128)}, s32[128]{0:T(128)S(1)}, u32[]{:S(2)}) copy-start(s32[128]{0:T(128)S(1)} %get-tuple-element.52) | copy-start | bytes 1540
  2.8 22.4 %copy-start.40 = (s32[128]{0:T(128)}, s32[128]{0:T(128)S(1)}, u32[]{:S(2)}) copy-start(s32[128]{0:T(128)S(1)} %get-tuple-element.51) | copy-start | bytes 1540
  2.8 22.4 %copy-start.36 = (s32[1024]{0:T(1024)}, s32[1024]{0:T(1024)S(1)}, u32[]{:S(2)}) copy-start(s32[1024]{0:T(1024)S(1)} %get-tuple-element.59) | copy-start | bytes 12292
  2.8 22.4 %copy-start.37 = (s32[1024]{0:T(1024)}, s32[1024]{0:T(1024)S(1)}, u32[]{:S(2)}) copy-start(s32[1024]{0:T(1024)S(1)} %get-tuple-element.58) | copy-start | bytes 12292
  4.3 52.1 %collective-permute-start.1 = (bf16[1,128,160]{2,1,0:T(8,128)(2,1)}, bf16[1,128,160]{2,1,0:T(8,128)(2,1)}, u32[]{:S(2)}, u32[]{:S(2)}) collective-permute-start(bf16[1,128,160]{2,1,0:T(8,128)(2,1)} %bitcast.13), channel_id=1, source_target_pairs={{1,0},{2,1},{3,2},{4,3},{5,4},{6,5},{7,6},{8,7},{9,8},{10,9},{11,1... | collective-permute-start | bytes 122888 | tf_op jit(solution)/shard_map/ppermute | solution.py:17
  7.7 49.8 %collective-permute-start = (bf16[1,128,160]{2,1,0:T(8,128)(2,1)}, bf16[1,128,160]{2,1,0:T(8,128)(2,1)}, u32[]{:S(2)}, u32[]{:S(2)}) collective-permute-start(bf16[1,128,160]{2,1,0:T(8,128)(2,1)} %bitcast.9), channel_id=1, source_target_pairs={{0,1},{1,2},{2,3},{3,4},{4,5},{5,6},{6,7},{7,8},{8,9},{9,10},{10,1... | collective-permute-start | bytes 122888 | tf_op jit(solution)/shard_map/ppermute | solution.py:15
  10.1 43.6 %copy-start.24 = (pred[32,32]{1,0:T(8,128)(4,1)}, pred[32,32]{1,0:T(8,128)(4,1)S(1)}, u32[]{:S(2)}) copy-start(pred[32,32]{1,0:T(8,128)(4,1)S(1)} %iota_compare_fusion.3) | copy-start | bytes 3076
  10.2 45.5 %copy-start.22 = (pred[32,32]{1,0:T(8,128)(4,1)}, pred[32,32]{1,0:T(8,128)(4,1)S(1)}, u32[]{:S(2)}) copy-start(pred[32,32]{1,0:T(8,128)(4,1)S(1)} %iota_compare_fusion.7) | copy-start | bytes 3076
  10.4 43.3 %copy-start.30 = (s32[1024]{0:T(1024)}, s32[1024]{0:T(1024)S(1)}, u32[]{:S(2)}) copy-start(s32[1024]{0:T(1024)S(1)} %pad_clamp_fusion.2) | copy-start | bytes 12292
  39.2 12.7 %copy-start.11 = (f32[8,32,32]{2,1,0:T(8,128)}, f32[8,32,32]{2,1,0:T(8,128)S(1)}, u32[]{:S(2)}) copy-start(f32[8,32,32]{2,1,0:T(8,128)S(1)} %all_gather.30) | copy-start | bytes 98308
  51.9 1.8 copy-start.5
  53.7 2.0 copy-start.16
  53.7 2.0 copy-start.42
  53.7 2.7 copy-start.9
  53.7 3.8 %copy-start.1 = (f32[768,160]{0,1:T(8,128)S(1)}, f32[768,160]{0,1:T(8,128)}, u32[]{:S(2)}) copy-start(f32[768,160]{0,1:T(8,128)} %param.20) | copy-start | bytes 1474564
  53.7 3.8 %copy-start.7 = (bf16[768,128]{1,0:T(8,128)(2,1)S(1)}, bf16[768,128]{1,0:T(8,128)(2,1)}, u32[]{:S(2)}) copy-start(bf16[768,128]{1,0:T(8,128)(2,1)} %param.24) | copy-start | bytes 589828
  53.7 3.8 %copy-start.12 = (f32[768,160]{0,1:T(8,128)S(1)}, f32[768,160]{0,1:T(8,128)}, u32[]{:S(2)}) copy-start(f32[768,160]{0,1:T(8,128)} %param.19) | copy-start | bytes 1474564
  53.7 3.8 %copy-start.32 = (f32[768]{0:T(1024)S(1)}, f32[768]{0:T(1024)}, u32[]{:S(2)}) copy-start(f32[768]{0:T(1024)} %param.21) | copy-start | bytes 9220
  56.4 46.9 %copy-start.13 = (f32[1,32,32]{2,1,0:T(8,128)}, f32[1,32,32]{2,1,0:T(8,128)S(1)}, u32[]{:S(2)}) copy-start(f32[1,32,32]{2,1,0:T(8,128)S(1)} %get-tuple-element.38) | copy-start | bytes 12292
  59.5 20.4 %slice-start.1 = ((f32[8,32,32]{2,1,0:T(8,128)}), f32[1,32,32]{2,1,0:T(8,128)S(1)}, s32[]{:S(2)}) async-start(f32[8,32,32]{2,1,0:T(8,128)} %copy-done.11), calls=%async_computation.1 | async-start | bytes 32768 | tf_op jit(solution)/shard_map/slice | solution.py:161
  59.6 30.7 %copy-start.20 = (bf16[1,1024,32]{1,2,0:T(8,128)(2,1)S(1)}, bf16[1,1024,32]{1,2,0:T(8,128)(2,1)}, u32[]{:S(2)}) copy-start(bf16[1,1024,32]{1,2,0:T(8,128)(2,1)} %param.28) | copy-start | bytes 196612
  61.8 27.9 %collective-permute-start.3 = (bf16[1,128,160]{1,2,0:T(8,128)(2,1)S(1)}, bf16[1,128,160]{1,2,0:T(8,128)(2,1)S(1)}, u32[]{:S(2)}, u32[]{:S(2)}) collective-permute-start(bf16[1,128,160]{1,2,0:T(8,128)(2,1)S(1)} %bitcast.412), channel_id=1, source_target_pairs={{1,0},{2,1},{3,2},{4,3},{5,4},{6,5},{7,6},{8,7},{9,8},{10,9},{11,1... | collective-permute-start | bytes 122888 | tf_op jit(solution)/shard_map/ppermute | solution.py:17
  65.9 23.7 %collective-permute-start.2 = (bf16[1,128,160]{1,2,0:T(8,128)(2,1)S(1)}, bf16[1,128,160]{1,2,0:T(8,128)(2,1)S(1)}, u32[]{:S(2)}, u32[]{:S(2)}) collective-permute-start(bf16[1,128,160]{1,2,0:T(8,128)(2,1)S(1)} %bitcast.413), channel_id=1, source_target_pairs={{0,1},{1,2},{2,3},{3,4},{4,5},{5,6},{6,7},{7,8},{8,9},{9,10},{10,1... | collective-permute-start | bytes 122888 | tf_op jit(solution)/shard_map/ppermute | solution.py:15
  90.3 13.0 %copy-start.18 = (f32[4,1,32,32]{2,3,1,0:T(8,128)S(1)}, f32[4,1,32,32]{2,3,1,0:T(8,128)}, u32[]{:S(2)}) copy-start(f32[4,1,32,32]{2,3,1,0:T(8,128)} %custom-call.48) | copy-start | bytes 49156
  90.3 13.1 %copy-start.19 = (f32[4,32,32]{2,1,0:T(8,128)S(1)}, f32[4,32,32]{2,1,0:T(8,128)}, u32[]{:S(2)}) copy-start(f32[4,32,32]{2,1,0:T(8,128)} %copy.187) | copy-start | bytes 49156
  104.5 7.3 %copy-start.25 = (pred[32,32]{1,0:T(8,128)(4,1)S(1)}, pred[32,32]{1,0:T(8,128)(4,1)}, u32[]{:S(2)}) copy-start(pred[32,32]{1,0:T(8,128)(4,1)} %copy-done.24) | copy-start | bytes 3076
  104.5 7.5 %copy-start.23 = (pred[32,32]{1,0:T(8,128)(4,1)S(1)}, pred[32,32]{1,0:T(8,128)(4,1)}, u32[]{:S(2)}) copy-start(pred[32,32]{1,0:T(8,128)(4,1)} %copy-done.22) | copy-start | bytes 3076
  134.6 1.9 slice-start
  135.2 33.1 %copy-start.44 = (pred[4]{0:T(512)(128)(4,1)S(1)}, pred[4]{0:T(512)(128)(4,1)}, u32[]{:S(2)}) copy-start(pred[4]{0:T(512)(128)(4,1)} %constant.263.clone.1) | copy-start | bytes 16
  152.4 32.1 %copy-start.17 = (f32[4,32,32]{1,2,0:T(8,128)S(1)}, f32[4,32,32]{1,2,0:T(8,128)}, u32[]{:S(2)}) copy-start(f32[4,32,32]{1,2,0:T(8,128)} %copy.210) | copy-start | bytes 49156
  212.5 1.7 copy-start.21
  215.4 4.7 %collective-permute-start.5 = (bf16[1,128,160]{1,2,0:T(8,128)(2,1)S(1)}, bf16[1,128,160]{1,2,0:T(8,128)(2,1)S(1)}, u32[]{:S(2)}, u32[]{:S(2)}) collective-permute-start(bf16[1,128,160]{1,2,0:T(8,128)(2,1)S(1)} %get-tuple-element.34), channel_id=1, source_target_pairs={{1,0},{2,1},{3,2},{4,3},{5,4},{6,5},{7,6},{8,7},{9,8},{10,9},{11,1... | collective-permute-start | bytes 122888 | tf_op jit(solution)/shard_map/ppermute | solution.py:17
  217.3 7.1 %collective-permute-start.4 = (bf16[1,128,160]{1,2,0:T(8,128)(2,1)S(1)}, bf16[1,128,160]{1,2,0:T(8,128)(2,1)S(1)}, u32[]{:S(2)}, u32[]{:S(2)}) collective-permute-start(bf16[1,128,160]{1,2,0:T(8,128)(2,1)S(1)} %get-tuple-element.33), channel_id=1, source_target_pairs={{0,1},{1,2},{2,3},{3,4},{4,5},{5,6},{6,7},{7,8},{8,9},{9,10},{10,1... | collective-permute-start | bytes 122888 | tf_op jit(solution)/shard_map/ppermute | solution.py:15
  219.8 4.8 %copy-start.41 = (s32[128]{0:T(128)S(1)}, s32[128]{0:T(128)}, u32[]{:S(2)}) copy-start(s32[128]{0:T(128)} %copy-done.40) | copy-start | bytes 1540
  224.5 1.7 copy-start.39
  228.9 7.1 %copy-start.31 = (s32[1024]{0:T(1024)S(1)}, s32[1024]{0:T(1024)}, u32[]{:S(2)}) copy-start(s32[1024]{0:T(1024)} %copy-done.30) | copy-start | bytes 12292
  231.4 6.9 %collective-permute-start.7 = (bf16[1,128,160]{2,1,0:T(8,128)(2,1)}, bf16[1,128,160]{2,1,0:T(8,128)(2,1)S(1)}, u32[]{:S(2)}, u32[]{:S(2)}) collective-permute-start(bf16[1,128,160]{2,1,0:T(8,128)(2,1)} %bitcast.124), channel_id=1, source_target_pairs={{1,0},{2,1},{3,2},{4,3},{5,4},{6,5},{7,6},{8,7},{9,8},{10,9},{11,1... | collective-permute-start | bytes 122888 | tf_op jit(solution)/shard_map/ppermute | solution.py:17
  233.4 8.3 %collective-permute-start.6 = (bf16[1,128,160]{2,1,0:T(8,128)(2,1)S(1)}, bf16[1,128,160]{2,1,0:T(8,128)(2,1)S(1)}, u32[]{:S(2)}, u32[]{:S(2)}) collective-permute-start(bf16[1,128,160]{2,1,0:T(8,128)(2,1)S(1)} %bitcast.407), channel_id=1, source_target_pairs={{0,1},{1,2},{2,3},{3,4},{4,5},{5,6},{6,7},{7,8},{8,9},{9,10},{10,1... | collective-permute-start | bytes 122888 | tf_op jit(solution)/shard_map/ppermute | solution.py:15
  236.7 1.6 copy-start.10
  236.7 4.9 %copy-start.3 = (f32[768,160]{0,1:T(8,128)S(1)}, f32[768,160]{0,1:T(8,128)}, u32[]{:S(2)}) copy-start(f32[768,160]{0,1:T(8,128)} %get-tuple-element.54) | copy-start | bytes 1474564
  236.7 4.9 %copy-start.4 = (f32[768,160]{0,1:T(8,128)S(1)}, f32[768,160]{0,1:T(8,128)}, u32[]{:S(2)}) copy-start(f32[768,160]{0,1:T(8,128)} %copy.230) | copy-start | bytes 1474564
  236.7 4.9 %copy-start.8 = (bf16[768,128]{1,0:T(8,128)(2,1)S(1)}, bf16[768,128]{1,0:T(8,128)(2,1)}, u32[]{:S(2)}) copy-start(bf16[768,128]{1,0:T(8,128)(2,1)} %param.24) | copy-start | bytes 589828
  236.8 4.9 %copy-start.33 = (f32[768]{0:T(1024)S(1)}, f32[768]{0:T(1024)}, u32[]{:S(2)}) copy-start(f32[768]{0:T(1024)} %param.21) | copy-start | bytes 9220
  241.7 45.2 %copy-start.2 = (f32[768,160]{0,1:T(8,128)S(1)}, f32[768,160]{0,1:T(8,128)}, u32[]{:S(2)}) copy-start(f32[768,160]{0,1:T(8,128)} %param.20) | copy-start | bytes 1474564
  (7 other events, 6.0 us)
where the time goes:
time: 290 us; the launch traced here: 289 us
  blocking collectives  142 us (49%)
  other arithmetic  79.4 us (27%)
  matrix products  21.8 us (8%)
  starting transfers between devices  18.9 us (7%)
  local copies, waits for them, and re-layouts  17.4 us (6%)
  waiting for transfers between devices  7.38 us (3%)
    psum x1, blocking collectives, shards(): inner = lax.psum(jnp.sum(residual_start * owned, axis=0), ('grp', 'sub'))  44.1 us
    another operation x15, other arithmetic, chol_solve(): lax.linalg.triangular_solve(factor, halfway, left_side=True, lower=True,...  34 us
    another operation x15, other arithmetic, solve_chain(): factor = jnp.linalg.cholesky(diag_odd)  31.6 us
    all_gather x1, blocking collectives, shards(): blocks_up = lax.all_gather(coarse_up, 'sub', axis=0, tiled=True)  14.8 us
    all_gather x1, blocking collectives, shards(): blocks_diag = lax.all_gather(coarse_diag, 'sub', axis=0, tiled=True)  14 us
    all_gather x1, blocking collectives, shards(): columns = lax.all_gather(coarse_in[None], 'sub', axis=0, tiled=True)  12.7 us
    ppermute x4, starting transfers between devices, with_halo(): lax.ppermute(head, axis, [((i + 1) % count, i) for i in range(ends)])  9.75 us
    ppermute x4, starting transfers between devices, with_halo(): lax.ppermute(tail, axis, [(i, (i + 1) % count) for i in range(ends)])  9.13 us
  transfers between devices with their start and end apart: 8, of which 2 were waited for; matrix products, arithmetic and copies ran while one was open for 12% of the time, Pallas kernels for 0%

commit v1 on v0

--- a/solution.py
+++ b/solution.py
@@ -133,8 +133,13 @@
     extended = jnp.concatenate([from_left, rounded, from_right], axis=0)
     local_part = jnp.dot(local_inverse[0], extended, preferred_element_type=f32)
     coarse_in = jnp.dot(coarse_basis[0].T, extended, preferred_element_type=f32)
-    blocks_diag = lax.all_gather(coarse_diag, "sub", axis=0, tiled=True)
-    blocks_up = lax.all_gather(coarse_up, "sub", axis=0, tiled=True)
+    blocks_diag, blocks_up = jnp.split(
+        lax.all_gather(
+            jnp.concatenate([coarse_diag, coarse_up], axis=1), "sub", axis=0, tiled=True
+        ),
+        [coarse_diag.shape[1]],
+        axis=1,
+    )
     group = lax.axis_index("grp")
     groups = lax.axis_size("grp")
     member = lax.axis_index("sub")

time: 290 us -> 277 us (0.955)
  blocking collectives: 142 us -> 128 us
    all_gather x2 -> x1, blocking collectives: 28.8 us -> 14.8 us  [shards(): lax.all_gather(jnp.concatenate([coarse_diag, coarse_up], axis=1), 'sub',...]
  transfers between devices with their start and end apart: 8 -> 8, of which waited for: 2 -> 2; matrix products, arithmetic and copies ran while one was open for 12% -> 13% of each run, Pallas kernels for 0% -> 0%
where the time goes in v1:
time: 277 us; the launch traced here: 276 us
  blocking collectives  128 us (46%)
  other arithmetic  78.4 us (28%)
  matrix products  23.9 us (9%)
  starting transfers between devices  19 us (7%)
  local copies, waits for them, and re-layouts  18.1 us (7%)
  waiting for transfers between devices  7.18 us (3%)
    psum x1, blocking collectives, shards(): inner = lax.psum(jnp.sum(residual_start * owned, axis=0), ('grp', 'sub'))  44 us
    another operation x15, other arithmetic, chol_solve(): lax.linalg.triangular_solve(factor, halfway, left_side=True, lower=True,...  33.4 us
    another operation x15, other arithmetic, solve_chain(): factor = jnp.linalg.cholesky(diag_odd)  31.1 us
    all_gather x1, blocking collectives, shards(): lax.all_gather(jnp.concatenate([coarse_diag, coarse_up], axis=1), 'sub',...  14.8 us
    all_gather x1, blocking collectives, shards(): columns = lax.all_gather(coarse_in[None], 'sub', axis=0, tiled=True)  12.6 us
    ppermute x4, starting transfers between devices, with_halo(): lax.ppermute(head, axis, [((i + 1) % count, i) for i in range(ends)])  9.74 us
    ppermute x4, starting transfers between devices, with_halo(): lax.ppermute(tail, axis, [(i, (i + 1) % count) for i in range(ends)])  9.26 us
    all_gather x1, blocking collectives, shards(): sep_diag = lax.all_gather(blocks_diag[0][None], 'grp', axis=0, tiled=True)  9.15 us
  transfers between devices with their start and end apart: 8, of which 2 were waited for; matrix products, arithmetic and copies ran while one was open for 13% of the time, Pallas kernels for 0%

profile of v1, /device:TPU:14, one launch (start us, length us, event | category | flops | bytes accessed | tf_op | source)
XLA Modules:
  0.0 276.5 jit_solution(5744152598723178158)
XLA Ops:
  0.7 1.3 copy.179
  2.8 1.5 gather_fusion.2
  4.3 1.9 collective-permute-start.1
  6.2 1.5 gather_fusion.1
  7.7 2.4 collective-permute-start
  10.4 14.8 %all_gather.27 = f32[8,64,32]{1,2,0:T(8,128)S(1)} all-gather(f32[1,64,32]{1,2,0:T(8,128)S(1)} %pad_maximum_fusion.14), channel_id=1, replica_groups=mesh['grp'=4,'sub'=8] {'sub'}, dimensions={0}, use_global_device_ids=true | all-gather | bytes 73728 | tf_op jit(solution)/shard_map/all_gather | solution.py:137
  26.4 11.7 %custom-call.47 = f32[4,32,32]{2,1,0:T(8,128)S(1)} custom-call(f32[4,32,32]{2,1,0:T(8,128)S(1)} %copy.192), custom_call_target="Cholesky" | custom-call | tf_op jit(solution)/shard_map/jit(cholesky)/cholesky | solution.py:55
  38.3 1.7 gather_fusion
  40.0 2.6 convolution_bitcast_fusion.1
  43.5 1.1 fusion.73
  44.6 2.3 fusion.214
  49.1 4.0 %collective-permute-start.3 = (bf16[1,128,160]{1,2,0:T(8,128)(2,1)S(1)}, bf16[1,128,160]{1,2,0:T(8,128)(2,1)S(1)}, u32[]{:S(2)}, u32[]{:S(2)}) collective-permute-start(bf16[1,128,160]{1,2,0:T(8,128)(2,1)S(1)} %bitcast.403), channel_id=1, source_target_pairs={{1,0},{2,1},{3,2},{4,3},{5,4},{6,5},{7,6},{8,7},{9,8},{10,9},{11,1... | collective-permute-start | bytes 122888 | tf_op jit(solution)/shard_map/ppermute | solution.py:17
  53.3 2.1 collective-permute-start.2
  56.0 10.5 %custom-call.48 = f32[4,1,32,32]{2,3,1,0:T(8,128)S(1)} custom-call(f32[4,1,32,32]{3,2,1,0:T(8,128)} %select_bitcast_fusion), custom_call_target="InvertDiagBlocksLowerTriangular" | custom-call | tf_op jit(solution)/shard_map/triangular_solve | solution.py:26
  66.7 9.2 %all_gather.28 = f32[4,32,32]{2,1,0:T(8,128)S(1)} all-gather(f32[1,32,32]{2,1,0:T(8,128)S(1)} %copy.189), channel_id=1, replica_groups=mesh['grp'=4,'sub'=8] {'grp'}, dimensions={0}, use_global_device_ids=true | all-gather | bytes 20480 | tf_op jit(solution)/shard_map/all_gather | solution.py:166
  77.4 12.6 %all-gather = f32[256,160]{1,0:T(8,128)S(1)} all-gather(f32[32,160]{1,0:T(8,128)S(1)} %convolution_bitcast_fusion.10), channel_id=2, replica_groups=mesh['grp'=4,'sub'=8] {'sub'}, dimensions={0}, use_global_device_ids=true | all-gather | bytes 184320 | tf_op jit(solution)/shard_map/all_gather | solution.py:150
  90.6 1.2 fusion.69
  93.6 5.9 %custom-call.57 = f32[2,32,32]{2,1,0:T(8,128)S(1)} custom-call(f32[2,32,32]{2,1,0:T(8,128)S(1)} %fusion.118), custom_call_target="Cholesky" | custom-call | tf_op jit(solution)/shard_map/jit(cholesky)/cholesky | solution.py:55
  99.7 4.9 %custom-call.49 = f32[2,1,32,32]{2,3,1,0:T(8,128)S(1)} custom-call(f32[2,1,32,32]{3,2,1,0:T(8,128)S(1)} %fusion.120), custom_call_target="InvertDiagBlocksLowerTriangular" | custom-call | tf_op jit(solution)/shard_map/triangular_solve | solution.py:26
  106.7 2.9 %custom-call.58 = f32[1,32,32]{2,1,0:T(8,128)S(1)} custom-call(f32[1,32,32]{2,1,0:T(8,128)S(1)} %fusion.169), custom_call_target="Cholesky" | custom-call | tf_op jit(solution)/shard_map/jit(cholesky)/cholesky | solution.py:55
  110.9 2.4 custom-call.50
  114.5 2.9 %cholesky.184 = f32[32,32]{1,0:T(8,128)S(1)} custom-call(f32[32,32]{1,0:T(8,128)S(1)} %fusion.150), custom_call_target="Cholesky" | custom-call | tf_op jit(solution)/shard_map/jit(cholesky)/cholesky | solution.py:74
  118.7 2.4 custom-call.51
  124.2 7.0 %all-gather.6 = f32[128,160]{1,0:T(8,128)S(1)} all-gather(f32[32,160]{1,0:T(8,128)S(1)} %slice-done), channel_id=8, replica_groups=mesh['grp'=4,'sub'=8] {'grp'}, dimensions={0}, use_global_device_ids=true | all-gather | bytes 102400 | tf_op jit(solution)/shard_map/all_gather | solution.py:167
  131.2 8.9 %all-gather.4 = f32[128,160]{1,0:T(8,128)S(1)} all-gather(f32[32,160]{1,0:T(8,128)S(1)} %fusion.102), channel_id=6, replica_groups=mesh['grp'=4,'sub'=8] {'grp'}, dimensions={0}, use_global_device_ids=true | all-gather | bytes 102400 | tf_op jit(solution)/shard_map/all_gather | solution.py:171
  140.2 7.3 %all-gather.5 = f32[128,160]{1,0:T(8,128)S(1)} all-gather(f32[32,160]{1,0:T(8,128)S(1)} %fusion.101), channel_id=7, replica_groups=mesh['grp'=4,'sub'=8] {'grp'}, dimensions={0}, use_global_device_ids=true | all-gather | bytes 102400 | tf_op jit(solution)/shard_map/all_gather | solution.py:172
  147.5 8.7 %all-gather.3 = f32[128,32]{1,0:T(8,128)S(1)} all-gather(f32[32,32]{1,0:T(8,128)S(1)} %fusion.146), channel_id=5, replica_groups=mesh['grp'=4,'sub'=8] {'grp'}, dimensions={0}, use_global_device_ids=true | all-gather | bytes 20480 | tf_op jit(solution)/shard_map/all_gather | solution.py:170
  156.4 6.8 %all-gather.2 = f32[128,32]{1,0:T(8,128)S(1)} all-gather(f32[32,32]{1,0:T(8,128)S(1)} %fusion.147), channel_id=4, replica_groups=mesh['grp'=4,'sub'=8] {'grp'}, dimensions={0}, use_global_device_ids=true | all-gather | bytes 20480 | tf_op jit(solution)/shard_map/all_gather | solution.py:169
  163.3 8.7 %all-gather.1 = f32[128,32]{1,0:T(8,128)S(1)} all-gather(f32[32,32]{1,0:T(8,128)S(1)} %fusion.148), channel_id=3, replica_groups=mesh['grp'=4,'sub'=8] {'grp'}, dimensions={0}, use_global_device_ids=true | all-gather | bytes 20480 | tf_op jit(solution)/shard_map/all_gather | solution.py:168
  172.2 5.9 %custom-call.59 = f32[2,32,32]{2,1,0:T(8,128)S(1)} custom-call(f32[2,32,32]{2,1,0:T(8,128)S(1)} %fusion.113), custom_call_target="Cholesky" | custom-call | tf_op jit(solution)/shard_map/jit(cholesky)/cholesky | solution.py:55
  178.3 4.9 %custom-call.52 = f32[2,1,32,32]{2,3,1,0:T(8,128)S(1)} custom-call(f32[2,1,32,32]{3,2,1,0:T(8,128)S(1)} %fusion.119), custom_call_target="InvertDiagBlocksLowerTriangular" | custom-call | tf_op jit(solution)/shard_map/triangular_solve | solution.py:26
  185.3 2.9 %custom-call.60 = f32[1,32,32]{2,1,0:T(8,128)S(1)} custom-call(f32[1,32,32]{2,1,0:T(8,128)S(1)} %fusion.158), custom_call_target="Cholesky" | custom-call | tf_op jit(solution)/shard_map/jit(cholesky)/cholesky | solution.py:55
  189.5 2.4 custom-call.53
  193.2 2.9 %cholesky.216 = f32[32,32]{1,0:T(8,128)S(1)} custom-call(f32[32,32]{1,0:T(8,128)S(1)} %fusion.149), custom_call_target="Cholesky" | custom-call | tf_op jit(solution)/shard_map/jit(cholesky)/cholesky | solution.py:74
  197.4 2.4 custom-call.54
  203.0 1.9 collective-permute-start.5
  204.9 2.4 collective-permute-start.4
  207.7 4.1 %collective-permute-done.4 = bf16[1,128,160]{1,2,0:T(8,128)(2,1)S(1)} collective-permute-done((bf16[1,128,160]{1,2,0:T(8,128)(2,1)S(1)}, bf16[1,128,160]{1,2,0:T(8,128)(2,1)S(1)}, u32[]{:S(2)}, u32[]{:S(2)}) %collective-permute-start.4) | collective-permute-done | bytes 40992 | tf_op jit(solution)/shard_map/ppermute | solution.py:15
  212.0 1.6 scatter_fusion
  213.6 1.6 scatter_fusion.1
  216.3 1.6 gather_fusion.7
  218.8 1.9 collective-permute-start.7
  220.8 2.4 collective-permute-start.6
  224.1 1.6 convolution_bitcast_fusion
  226.0 3.1 %collective-permute-done.6 = bf16[1,128,160]{2,1,0:T(8,128)(2,1)S(1)} collective-permute-done((bf16[1,128,160]{2,1,0:T(8,128)(2,1)S(1)}, bf16[1,128,160]{2,1,0:T(8,128)(2,1)S(1)}, u32[]{:S(2)}, u32[]{:S(2)}) %collective-permute-start.6) | collective-permute-done | bytes 40992 | tf_op jit(solution)/shard_map/ppermute | solution.py:15
  229.1 1.1 multiply_reduce_fusion
  230.2 44.0 %all-reduce.16 = (f32[160]{0:T(256)S(1)}, f32[160]{0:T(256)S(1)}) all-reduce(f32[160]{0:T(256)S(1)} %get-tuple-element.30, f32[160]{0:T(256)S(1)} %get-tuple-element.29), channel_id=1, replica_groups=mesh['grp'=4,'sub'=8] {'grp','sub'}, use_global_device_ids=true, to_apply=%region_11.15 | all-reduce | flops 320 | bytes 2560 | tf_op jit(solution)/shard_map/psum | solution.py:196
  274.2 2.3 multiply_subtract_fusion
  (246 shorter events, 32.3 us)
Async XLA Ops:
  0.6 201.5 %copy-start = (bf16[1,1024,1024]{2,1,0:T(8,128)(2,1)S(1)}, bf16[1,1024,1024]{2,1,0:T(8,128)(2,1)}, u32[]{:S(2)}) copy-start(bf16[1,1024,1024]{2,1,0:T(8,128)(2,1)} %param.27) | copy-start | bytes 6291460
  0.6 9.5 %copy-start.25 = (f32[1,32,32]{2,1,0:T(8,128)S(1)}, f32[1,32,32]{2,1,0:T(8,128)}, u32[]{:S(2)}) copy-start(f32[1,32,32]{2,1,0:T(8,128)} %param.30) | copy-start | bytes 12292
  0.7 9.6 %copy-start.26 = (f32[1,32,32]{2,1,0:T(8,128)S(1)}, f32[1,32,32]{2,1,0:T(8,128)}, u32[]{:S(2)}) copy-start(f32[1,32,32]{2,1,0:T(8,128)} %param.29) | copy-start | bytes 12292
  0.7 25.2 %copy-start.33 = (s32[1,6,3]{1,0,2:T(1,128)S(1)}, s32[1,6,3]{1,0,2:T(1,128)}, u32[]{:S(2)}) copy-start(s32[1,6,3]{1,0,2:T(1,128)} %param.23) | copy-start | bytes 220
  2.8 7.3 %copy-start.29 = (s32[128]{0:T(128)}, s32[128]{0:T(128)S(1)}, u32[]{:S(2)}) copy-start(s32[128]{0:T(128)S(1)} %get-tuple-element.53) | copy-start | bytes 1540
  2.8 7.3 %copy-start.31 = (s32[128]{0:T(128)}, s32[128]{0:T(128)S(1)}, u32[]{:S(2)}) copy-start(s32[128]{0:T(128)S(1)} %get-tuple-element.52) | copy-start | bytes 1540
  2.8 7.3 %copy-start.27 = (s32[1024]{0:T(1024)}, s32[1024]{0:T(1024)S(1)}, u32[]{:S(2)}) copy-start(s32[1024]{0:T(1024)S(1)} %get-tuple-element.60) | copy-start | bytes 12292
  2.8 7.3 %copy-start.28 = (s32[1024]{0:T(1024)}, s32[1024]{0:T(1024)S(1)}, u32[]{:S(2)}) copy-start(s32[1024]{0:T(1024)S(1)} %get-tuple-element.59) | copy-start | bytes 12292
  4.3 39.2 %collective-permute-start.1 = (bf16[1,128,160]{2,1,0:T(8,128)(2,1)}, bf16[1,128,160]{2,1,0:T(8,128)(2,1)}, u32[]{:S(2)}, u32[]{:S(2)}) collective-permute-start(bf16[1,128,160]{2,1,0:T(8,128)(2,1)} %bitcast.13), channel_id=1, source_target_pairs={{1,0},{2,1},{3,2},{4,3},{5,4},{6,5},{7,6},{8,7},{9,8},{10,9},{11,1... | collective-permute-start | bytes 122888 | tf_op jit(solution)/shard_map/ppermute | solution.py:17
  7.7 36.9 %collective-permute-start = (bf16[1,128,160]{2,1,0:T(8,128)(2,1)}, bf16[1,128,160]{2,1,0:T(8,128)(2,1)}, u32[]{:S(2)}, u32[]{:S(2)}) collective-permute-start(bf16[1,128,160]{2,1,0:T(8,128)(2,1)} %bitcast.9), channel_id=1, source_target_pairs={{0,1},{1,2},{2,3},{3,4},{4,5},{5,6},{6,7},{7,8},{8,9},{9,10},{10,1... | collective-permute-start | bytes 122888 | tf_op jit(solution)/shard_map/ppermute | solution.py:15
  26.2 12.1 %copy-start.7 = (f32[8,32,32]{1,2,0:T(8,128)}, f32[8,32,32]{1,2,0:T(8,128)S(1)}, u32[]{:S(2)}) copy-start(f32[8,32,32]{1,2,0:T(8,128)S(1)} %pad_maximum_fusion.4) | copy-start | bytes 98308
  38.3 1.7 copy-start.5
  40.0 3.5 %copy-start.11 = (bf16[768,128]{1,0:T(8,128)(2,1)S(1)}, bf16[768,128]{1,0:T(8,128)(2,1)}, u32[]{:S(2)}) copy-start(bf16[768,128]{1,0:T(8,128)(2,1)} %param.25) | copy-start | bytes 589828
  42.6 2.0 copy-start.1
  42.6 2.0 copy-start.9
  42.6 2.0 copy-start.24
  46.9 19.7 %copy-start.19 = (f32[1,32,32]{1,2,0:T(8,128)S(1)}, f32[1,32,32]{1,2,0:T(8,128)}, u32[]{:S(2)}) copy-start(f32[1,32,32]{1,2,0:T(8,128)} %get-tuple-element.37) | copy-start | bytes 12292
  46.9 30.3 %copy-start.16 = (bf16[1,1024,32]{1,2,0:T(8,128)(2,1)S(1)}, bf16[1,1024,32]{1,2,0:T(8,128)(2,1)}, u32[]{:S(2)}) copy-start(bf16[1,1024,32]{1,2,0:T(8,128)(2,1)} %param.28) | copy-start | bytes 196612
  49.1 27.4 %collective-permute-start.3 = (bf16[1,128,160]{1,2,0:T(8,128)(2,1)S(1)}, bf16[1,128,160]{1,2,0:T(8,128)(2,1)S(1)}, u32[]{:S(2)}, u32[]{:S(2)}) collective-permute-start(bf16[1,128,160]{1,2,0:T(8,128)(2,1)S(1)} %bitcast.403), channel_id=1, source_target_pairs={{1,0},{2,1},{3,2},{4,3},{5,4},{6,5},{7,6},{8,7},{9,8},{10,9},{11,1... | collective-permute-start | bytes 122888 | tf_op jit(solution)/shard_map/ppermute | solution.py:17
  53.3 36.7 %copy-start.18 = (f32[1,32,32]{2,1,0:T(8,128)S(1)}, f32[1,32,32]{2,1,0:T(8,128)}, u32[]{:S(2)}) copy-start(f32[1,32,32]{2,1,0:T(8,128)} %get-tuple-element.38) | copy-start | bytes 12292
  53.3 23.3 %collective-permute-start.2 = (bf16[1,128,160]{1,2,0:T(8,128)(2,1)S(1)}, bf16[1,128,160]{1,2,0:T(8,128)(2,1)S(1)}, u32[]{:S(2)}, u32[]{:S(2)}) collective-permute-start(bf16[1,128,160]{1,2,0:T(8,128)(2,1)S(1)} %bitcast.404), channel_id=1, source_target_pairs={{0,1},{1,2},{2,3},{3,4},{4,5},{5,6},{6,7},{7,8},{8,9},{9,10},{10,1... | collective-permute-start | bytes 122888 | tf_op jit(solution)/shard_map/ppermute | solution.py:15
  66.6 23.5 %copy-start.14 = (f32[4,1,32,32]{2,3,1,0:T(8,128)}, f32[4,1,32,32]{2,3,1,0:T(8,128)S(1)}, u32[]{:S(2)}) copy-start(f32[4,1,32,32]{2,3,1,0:T(8,128)S(1)} %custom-call.48) | copy-start | bytes 49156
  76.6 0.6 copy-start.20
  76.6 0.6 copy-start.22
  77.2 12.9 %copy-start.15 = (f32[4,32,32]{2,1,0:T(8,128)S(1)}, f32[4,32,32]{2,1,0:T(8,128)}, u32[]{:S(2)}) copy-start(f32[4,32,32]{2,1,0:T(8,128)} %copy.194) | copy-start | bytes 49156
  89.9 1.8 copy-start.6
  90.6 2.6 copy-start.8
  122.2 2.0 slice-start
  122.9 33.4 %copy-start.34 = (pred[4]{0:T(512)(128)(4,1)S(1)}, pred[4]{0:T(512)(128)(4,1)}, u32[]{:S(2)}) copy-start(pred[4]{0:T(512)(128)(4,1)} %constant.263.clone.1) | copy-start | bytes 16
  140.2 31.9 %copy-start.13 = (f32[4,32,32]{1,2,0:T(8,128)S(1)}, f32[4,32,32]{1,2,0:T(8,128)}, u32[]{:S(2)}) copy-start(f32[4,32,32]{1,2,0:T(8,128)} %copy.216) | copy-start | bytes 49156
  200.1 1.7 copy-start.17
  200.9 1.2 copy-start.21
  200.9 1.2 copy-start.23
  203.0 4.7 %collective-permute-start.5 = (bf16[1,128,160]{1,2,0:T(8,128)(2,1)S(1)}, bf16[1,128,160]{1,2,0:T(8,128)(2,1)S(1)}, u32[]{:S(2)}, u32[]{:S(2)}) collective-permute-start(bf16[1,128,160]{1,2,0:T(8,128)(2,1)S(1)} %get-tuple-element.34), channel_id=1, source_target_pairs={{1,0},{2,1},{3,2},{4,3},{5,4},{6,5},{7,6},{8,7},{9,8},{10,9},{11,1... | collective-permute-start | bytes 122888 | tf_op jit(solution)/shard_map/ppermute | solution.py:17
  204.9 6.8 %collective-permute-start.4 = (bf16[1,128,160]{1,2,0:T(8,128)(2,1)S(1)}, bf16[1,128,160]{1,2,0:T(8,128)(2,1)S(1)}, u32[]{:S(2)}, u32[]{:S(2)}) collective-permute-start(bf16[1,128,160]{1,2,0:T(8,128)(2,1)S(1)} %get-tuple-element.33), channel_id=1, source_target_pairs={{0,1},{1,2},{2,3},{3,4},{4,5},{5,6},{6,7},{7,8},{8,9},{9,10},{10,1... | collective-permute-start | bytes 122888 | tf_op jit(solution)/shard_map/ppermute | solution.py:15
  207.4 4.6 %copy-start.32 = (s32[128]{0:T(128)S(1)}, s32[128]{0:T(128)}, u32[]{:S(2)}) copy-start(s32[128]{0:T(128)} %copy-done.31) | copy-start | bytes 1540
  211.9 1.7 copy-start.30
  218.8 6.9 %collective-permute-start.7 = (bf16[1,128,160]{2,1,0:T(8,128)(2,1)}, bf16[1,128,160]{2,1,0:T(8,128)(2,1)S(1)}, u32[]{:S(2)}, u32[]{:S(2)}) collective-permute-start(bf16[1,128,160]{2,1,0:T(8,128)(2,1)} %bitcast.121), channel_id=1, source_target_pairs={{1,0},{2,1},{3,2},{4,3},{5,4},{6,5},{7,6},{8,7},{9,8},{10,9},{11,1... | collective-permute-start | bytes 122888 | tf_op jit(solution)/shard_map/ppermute | solution.py:17
  220.8 8.3 %collective-permute-start.6 = (bf16[1,128,160]{2,1,0:T(8,128)(2,1)S(1)}, bf16[1,128,160]{2,1,0:T(8,128)(2,1)S(1)}, u32[]{:S(2)}, u32[]{:S(2)}) collective-permute-start(bf16[1,128,160]{2,1,0:T(8,128)(2,1)S(1)} %bitcast.398), channel_id=1, source_target_pairs={{0,1},{1,2},{2,3},{3,4},{4,5},{5,6},{6,7},{7,8},{8,9},{9,10},{10,1... | collective-permute-start | bytes 122888 | tf_op jit(solution)/shard_map/ppermute | solution.py:15
  224.1 1.6 copy-start.12
  224.1 4.9 %copy-start.3 = (f32[768,160]{0,1:T(8,128)S(1)}, f32[768,160]{0,1:T(8,128)}, u32[]{:S(2)}) copy-start(f32[768,160]{0,1:T(8,128)} %get-tuple-element.55) | copy-start | bytes 1474564
  224.1 4.9 %copy-start.4 = (f32[768,160]{0,1:T(8,128)S(1)}, f32[768,160]{0,1:T(8,128)}, u32[]{:S(2)}) copy-start(f32[768,160]{0,1:T(8,128)} %copy.235) | copy-start | bytes 1474564
  224.1 4.9 %copy-start.10 = (bf16[768,128]{1,0:T(8,128)(2,1)S(1)}, bf16[768,128]{1,0:T(8,128)(2,1)}, u32[]{:S(2)}) copy-start(bf16[768,128]{1,0:T(8,128)(2,1)} %param.24) | copy-start | bytes 589828
  229.0 45.1 %copy-start.2 = (f32[768,160]{0,1:T(8,128)S(1)}, f32[768,160]{0,1:T(8,128)}, u32[]{:S(2)}) copy-start(f32[768,160]{0,1:T(8,128)} %param.20) | copy-start | bytes 1474564
